TPU v7x, 32 devices: a whole 2x2x4 slice. The times are simulated.
32 devices in a mesh: dp: 16 (over z, y, x), fsdp: 2 (over core).
Axes of the slice: x: 2, y: 2, z: 4, core: 2. Of those that a mesh axis runs over, the one named last changes fastest.
Arguments:
- tokens: bfloat16 [64, 512, 768], P(('dp', 'fsdp')), may hold values from -6 to 6
- cotangent: bfloat16 [64, 80, 768], P(('dp', 'fsdp')), may hold values from -6 to 6
- positions: int32 [64, 80], P(('dp', 'fsdp')), may hold values from 0 to 511, as said below
- counts: int32 [64], P(('dp', 'fsdp')), may hold values from 40 to 80
- query_key_value_weight: bfloat16 [2, 768, 2304], P(None, ('dp', 'fsdp')), may hold values from -0.21875 to 0.21875
- attention_output_weight: bfloat16 [2, 768, 768], P(None, ('dp', 'fsdp')), may hold values from -0.625 to 0.625
- feedforward_input_weight: bfloat16 [2, 768, 3072], P(None, ('dp', 'fsdp')), may hold values from -0.21875 to 0.21875
- feedforward_input_bias: bfloat16 [2, 3072], P(None, ('dp', 'fsdp')), may hold values from -3 to 3
- feedforward_output_weight: bfloat16 [2, 3072, 768], P(None, ('dp', 'fsdp')), may hold values from -0.109375 to 0.109375
- small: bfloat16 [2, 768, 24], P(None, ('dp', 'fsdp'))
- query_up_weight: float32 [2, 8, 768], replicated, may hold values from -1.2 to 1.2
- value_up_weight: float32 [2, 8, 768], replicated, may hold values from -1.2 to 1.2
Outputs:
- activations: bfloat16 [64, 512, 768], P(('dp', 'fsdp'))
- d_tokens: float32 [64, 512, 768], P(('dp', 'fsdp'))
- query_up_gradient: float32 [2, 8, 768], replicated
- value_up_gradient: float32 [2, 8, 768], replicated
Inputs may be any that keep to these rules, and one draw needn't show every extreme that they name: In each sequence the 80 entries are distinct positions; entry m is used where m < counts of that sequence.
All inputs are finite; a program needn't handle non-finite values.
Results may differ from a plain program's by a relative error of at most 0.03.
Values may be sent and summed in bfloat16 or wider, within the bound.
No kernel may reach another device: no remote copies, remote signals or barrier semaphores. Data moves between devices by JAX's collectives and lax.ppermute only.
A program may use at most 256 MiB of HBM per device.

v0:
```python
import jax
import jax.numpy as jnp
from jax import lax
from jax.sharding import PartitionSpec as P

MODEL_WIDTH = 768
H = 12
HD = 64
ADAPTER_RANK = 8
ENCODER_LAYERS = 2
LEN = 512
MAXM = 80
EPSILON = 1e-05


def layer_norm(value, norm_gain, norm_shift):
    average = jnp.mean(value, axis=-1, keepdims=True)
    centred = value - average
    spread = jnp.mean(centred * centred, axis=-1, keepdims=True)
    return centred * lax.rsqrt(spread + EPSILON) * norm_gain + norm_shift


def gelu_exact(value):
    return jax.nn.gelu(value, approximate=False)


def matrix_multiply(left, right):
    return jnp.dot(left, right, preferred_element_type=jnp.float32)


def transposed_multiply(left, right):
    return lax.dot_general(
        left, right, (((1,), (1,)), ((), ())), preferred_element_type=jnp.float32
    )


def leading_axis_contract(left, right):
    return lax.dot_general(
        left, right, (((0,), (0,)), ((), ())), preferred_element_type=jnp.float32
    )


def fetch_forward(layer_qkv, layer_o, layer_in, layer_bias, layer_out, layer_small):
    return (
        lax.all_gather(layer_qkv, ("dp", "fsdp"), axis=0, tiled=True),
        lax.all_gather(layer_o, ("dp", "fsdp"), axis=0, tiled=True),
        lax.all_gather(layer_in, ("dp", "fsdp"), axis=0, tiled=True),
        lax.all_gather(layer_bias, ("dp", "fsdp"), axis=0, tiled=True),
        lax.all_gather(layer_out, ("dp", "fsdp"), axis=0, tiled=True),
        lax.all_gather(layer_small, ("dp", "fsdp"), axis=0, tiled=True),
    )


def fetch_backward(layer_qkv, layer_o, layer_in, layer_bias, layer_out, layer_small):
    return (
        lax.all_gather(layer_qkv, ("dp", "fsdp"), axis=0, tiled=True),
        lax.all_gather(layer_o, ("dp", "fsdp"), axis=0, tiled=True),
        lax.all_gather(layer_in, ("dp", "fsdp"), axis=0, tiled=True),
        lax.all_gather(layer_bias, ("dp", "fsdp"), axis=0, tiled=True),
        lax.all_gather(layer_out, ("dp", "fsdp"), axis=0, tiled=True),
        lax.all_gather(layer_small, ("dp", "fsdp"), axis=0, tiled=True),
    )


def attend(packed_projection):
    heads_view = packed_projection.reshape(LEN, 3, H, HD)
    query_rows = heads_view[:, 0]
    key_rows = heads_view[:, 1]
    value_matrix_rows = heads_view[:, 2]
    scores = (
        jnp.einsum("qhd,khd->hqk", query_rows, key_rows, preferred_element_type=jnp.float32) * 0.125
    )
    row_max = jnp.max(scores, axis=-1, keepdims=True)
    powers = jnp.exp(scores - row_max)
    row_sum = jnp.sum(powers, axis=-1, keepdims=True)
    soft_probs = (powers / row_sum).astype(jnp.bfloat16)
    context = jnp.einsum(
        "hqk,khd->qhd", soft_probs, value_matrix_rows, preferred_element_type=jnp.float32
    )
    return (
        context.reshape(LEN, H * HD).astype(jnp.bfloat16),
        (row_max + jnp.log(row_sum))[:, :, 0],
    )


def attend_back(element):
    packed_projection, logsumexp_total, d_context = element
    heads_view = packed_projection.reshape(LEN, 3, H, HD)
    query_rows = heads_view[:, 0]
    key_rows = heads_view[:, 1]
    value_matrix_rows = heads_view[:, 2]
    grad_view = d_context.reshape(LEN, H, HD)
    scores = (
        jnp.einsum("qhd,khd->hqk", query_rows, key_rows, preferred_element_type=jnp.float32) * 0.125
    )
    soft_probs = jnp.exp(scores - logsumexp_total[:, :, None])
    d_probs = jnp.einsum(
        "qhd,khd->hqk", grad_view, value_matrix_rows, preferred_element_type=jnp.float32
    )
    d_scores = (
        soft_probs * (d_probs - jnp.sum(soft_probs * d_probs, axis=-1, keepdims=True))
    ).astype(jnp.bfloat16)
    d_queries = (
        jnp.einsum("hqk,khd->qhd", d_scores, key_rows, preferred_element_type=jnp.float32) * 0.125
    ).astype(jnp.bfloat16)
    d_keys = (
        jnp.einsum("hqk,qhd->khd", d_scores, query_rows, preferred_element_type=jnp.float32) * 0.125
    ).astype(jnp.bfloat16)
    d_values = jnp.einsum(
        "hqk,qhd->khd",
        soft_probs.astype(jnp.bfloat16),
        grad_view,
        preferred_element_type=jnp.float32,
    ).astype(jnp.bfloat16)
    return jnp.stack([d_queries, d_keys, d_values], axis=1).reshape(LEN, 3 * H * HD)


def layer_forward_pass(hidden_state, collected_rows, query_adapter_output, value_adapter_output):
    (
        query_key_value_weight,
        attention_output_weight,
        feedforward_input_weight,
        feedforward_input_bias,
        feedforward_output_weight,
        small,
    ) = collected_rows
    params = small.astype(jnp.float32)
    rounded_input = hidden_state.astype(jnp.bfloat16)
    adapter_down_weight = matrix_multiply(rounded_input, small[:, 8 : 8 + 2 * ADAPTER_RANK]).astype(
        jnp.bfloat16
    )
    adapter_up_weight = jnp.concatenate(
        [
            2.0
            * matrix_multiply(
                adapter_down_weight[:, :ADAPTER_RANK], query_adapter_output.astype(jnp.bfloat16)
            ),
            jnp.zeros_like(hidden_state),
            2.0
            * matrix_multiply(
                adapter_down_weight[:, ADAPTER_RANK:], value_adapter_output.astype(jnp.bfloat16)
            ),
        ],
        axis=1,
    )
    bias_vector_row = jnp.concatenate([params[:, 0], jnp.zeros_like(params[:, 0]), params[:, 1]])
    packed_projection = (
        matrix_multiply(rounded_input, query_key_value_weight) + bias_vector_row + adapter_up_weight
    ).astype(jnp.bfloat16)
    context, logsumexp_total = lax.map(attend, packed_projection.reshape(-1, LEN, 3 * MODEL_WIDTH))
    context = context.reshape(-1, MODEL_WIDTH)
    leading_partial_sum = hidden_state + (
        matrix_multiply(context, attention_output_weight) + params[:, 2]
    )
    normed = layer_norm(leading_partial_sum, params[:, 3], params[:, 4])
    preactivation_input = matrix_multiply(
        normed.astype(jnp.bfloat16), feedforward_input_weight
    ) + feedforward_input_bias.astype(jnp.float32)
    trailing_partial_sum = normed + (
        matrix_multiply(
            gelu_exact(preactivation_input).astype(jnp.bfloat16), feedforward_output_weight
        )
        + params[:, 5]
    )
    layer_output = layer_norm(trailing_partial_sum, params[:, 6], params[:, 7])
    return (
        layer_output,
        (
            packed_projection,
            adapter_down_weight,
            logsumexp_total,
            leading_partial_sum,
            preactivation_input,
            trailing_partial_sum,
        ),
    )


def layer_backward_pass(
    incoming_gradient, saved_state, collected_rows, query_adapter_output, value_adapter_output
):
    (
        query_key_value_weight,
        attention_output_weight,
        feedforward_input_weight,
        feedforward_input_bias,
        feedforward_output_weight,
        small,
    ) = collected_rows
    params = small.astype(jnp.float32)
    (
        packed_projection,
        adapter_down_weight,
        logsumexp_total,
        leading_partial_sum,
        preactivation_input,
        trailing_partial_sum,
    ) = saved_state
    unused_second, second_back = jax.vjp(
        lambda value: layer_norm(value, params[:, 6], params[:, 7]), trailing_partial_sum
    )
    d_second = second_back(incoming_gradient)[0]
    d_act = transposed_multiply(d_second.astype(jnp.bfloat16), feedforward_output_weight)
    unused_gelu, gelu_back = jax.vjp(gelu_exact, preactivation_input)
    d_pre = gelu_back(d_act)[0].astype(jnp.bfloat16)
    d_normed = d_second + transposed_multiply(d_pre, feedforward_input_weight)
    unused_first, first_back = jax.vjp(
        lambda value: layer_norm(value, params[:, 3], params[:, 4]), leading_partial_sum
    )
    d_first = first_back(d_normed)[0]
    d_context = transposed_multiply(d_first.astype(jnp.bfloat16), attention_output_weight).astype(
        jnp.bfloat16
    )
    d_packed = lax.map(
        attend_back,
        (
            packed_projection.reshape(-1, LEN, 3 * MODEL_WIDTH),
            logsumexp_total,
            d_context.reshape(-1, LEN, MODEL_WIDTH),
        ),
    )
    d_packed = d_packed.reshape(-1, 3 * MODEL_WIDTH)
    query_adapter_gradient = d_packed[:, :MODEL_WIDTH]
    value_adapter_gradient = d_packed[:, 2 * MODEL_WIDTH :]
    d_down = jnp.concatenate(
        [
            2.0
            * transposed_multiply(
                query_adapter_gradient, query_adapter_output.astype(jnp.bfloat16)
            ),
            2.0
            * transposed_multiply(
                value_adapter_gradient, value_adapter_output.astype(jnp.bfloat16)
            ),
        ],
        axis=1,
    ).astype(jnp.bfloat16)
    query_gradient_total = 2.0 * leading_axis_contract(
        adapter_down_weight[:, :ADAPTER_RANK], query_adapter_gradient
    )
    value_gradient_total = 2.0 * leading_axis_contract(
        adapter_down_weight[:, ADAPTER_RANK:], value_adapter_gradient
    )
    d_input = (
        d_first
        + transposed_multiply(d_packed, query_key_value_weight)
        + transposed_multiply(d_down, small[:, 8 : 8 + 2 * ADAPTER_RANK])
    )
    return (d_input, query_gradient_total, value_gradient_total)


def on_device(
    tokens,
    cotangent,
    positions,
    counts,
    query_key_value_weight,
    attention_output_weight,
    feedforward_input_weight,
    feedforward_input_bias,
    feedforward_output_weight,
    small,
    query_up_weight,
    value_up_weight,
):
    hidden_state = tokens.reshape(-1, MODEL_WIDTH).astype(jnp.float32)
    saved_state_stack = []
    gathered_all = []
    for layer_index in range(ENCODER_LAYERS):
        collected_rows = fetch_forward(
            query_key_value_weight[layer_index],
            attention_output_weight[layer_index],
            feedforward_input_weight[layer_index],
            feedforward_input_bias[layer_index],
            feedforward_output_weight[layer_index],
            small[layer_index],
        )
        hidden_state, saved_state = layer_forward_pass(
            hidden_state, collected_rows, query_up_weight[layer_index], value_up_weight[layer_index]
        )
        saved_state_stack.append(saved_state)
        gathered_all.append(collected_rows)
    activations = hidden_state.astype(jnp.bfloat16).reshape(tokens.shape)
    is_live = jnp.arange(MAXM)[None, :] < counts[:, None]
    indicator_matrix = (
        (positions[:, :, None] == jnp.arange(LEN)[None, None, :]) & is_live[:, :, None]
    ).astype(jnp.bfloat16)
    incoming_gradient = jnp.einsum(
        "nkw,nkq->nwq", indicator_matrix, cotangent, preferred_element_type=jnp.float32
    ).reshape(-1, MODEL_WIDTH)
    query_gradient_stack = [None] * ENCODER_LAYERS
    value_gradient_stack = [None] * ENCODER_LAYERS
    for layer_index in reversed(range(ENCODER_LAYERS)):
        collected_rows = fetch_backward(
            query_key_value_weight[layer_index],
            attention_output_weight[layer_index],
            feedforward_input_weight[layer_index],
            feedforward_input_bias[layer_index],
            feedforward_output_weight[layer_index],
            small[layer_index],
        )
        incoming_gradient, query_gradient_total, value_gradient_total = layer_backward_pass(
            incoming_gradient,
            saved_state_stack[layer_index],
            collected_rows,
            query_up_weight[layer_index],
            value_up_weight[layer_index],
        )
        query_gradient_total, value_gradient_total = lax.psum(
            (query_gradient_total, value_gradient_total), ("dp", "fsdp")
        )
        query_gradient_stack[layer_index] = query_gradient_total
        value_gradient_stack[layer_index] = value_gradient_total
    query_up_gradient = jnp.stack(query_gradient_stack)
    value_up_gradient = jnp.stack(value_gradient_stack)
    return (
        activations,
        incoming_gradient.reshape(tokens.shape),
        query_up_gradient,
        value_up_gradient,
    )


def solution(mesh):
    in_specs = (
        P(("dp", "fsdp"), None, None),
        P(("dp", "fsdp"), None, None),
        P(("dp", "fsdp"), None),
        P(("dp", "fsdp")),
        P(None, ("dp", "fsdp"), None),
        P(None, ("dp", "fsdp"), None),
        P(None, ("dp", "fsdp"), None),
        P(None, ("dp", "fsdp")),
        P(None, ("dp", "fsdp"), None),
        P(None, ("dp", "fsdp"), None),
        P(),
        P(),
    )
    out_specs = (P(("dp", "fsdp"), None, None), P(("dp", "fsdp"), None, None), P(), P())
    return jax.shard_map(
        on_device, mesh=mesh, in_specs=in_specs, out_specs=out_specs, check_vma=False
    )
```

profile of v0, /device:TPU:8, one launch (start us, length us, event | category | flops | bytes accessed | tf_op | source)
XLA Modules:
  0.0 912.4 jit_solution(5408790582590353400)
XLA Ops:
  17.6 36.0 %all-gather.7 = bf16[1,768,24]{2,1,0:T(8,128)(2,1)S(1)} all-gather(bf16[1,24,24]{2,1,0:T(8,128)(2,1)S(1)} %get-tuple-element.249), channel_id=9, replica_groups=mesh['dp'=16,'fsdp'=2] {'dp','fsdp'}, dimensions={1}, use_global_device_ids=true | all-gather | bytes 38016 | tf_op jit(solution)/shard_map/all_gather | solution.py:50
  56.3 37.5 %all-gather.1 = bf16[1,768,24]{2,1,0:T(8,128)(2,1)S(1)} all-gather(bf16[1,24,24]{2,1,0:T(8,128)(2,1)S(1)} %get-tuple-element.250), channel_id=3, replica_groups=mesh['dp'=16,'fsdp'=2] {'dp','fsdp'}, dimensions={1}, use_global_device_ids=true | all-gather | bytes 38016 | tf_op jit(solution)/shard_map/all_gather | solution.py:50
  99.7 45.6 %all-reduce.3 = (bf16[3072]{0:T(1024)(128)(2,1)S(1)}, bf16[3072]{0:T(1024)(128)(2,1)S(1)}) all-reduce(bf16[3072]{0:T(1024)(128)(2,1)S(1)} %dynamic-update-slice, bf16[3072]{0:T(1024)(128)(2,1)S(1)} %dynamic-update-slice.1), channel_id=6, replica_groups=mesh['dp'=16,'fsdp'=2] {'dp','fsdp'}, use_global_device_ids=true, to_apply=%add | all-reduce | flops 6144 | bytes 24576
  149.0 9.4 %fusion.54 = bf16[1024,2304]{1,0:T(8,128)(2,1)} fusion(f32[1024,768]{1,0:T(8,128)S(1)} %convolution_multiply_fusion.2, f32[1024,768]{1,0:T(8,128)} %convolution_multiply_fusion.3, bf16[1024,768]{1,0:T(8,128)(2,1)} %bitcast.377, f32[2304]{0:T(1024)S(1)} %get-tuple-element.255, f32[2304]{0:T(1024)S(1)} %get-tuple-element.254, ...), kind=kOutput, calls=%fused_computation.111 | convolution fusion | flops 3635675136 | bytes 16140288 | tf_op jit(solution)/shard_map/dot_general | solution.py:28
  158.4 6.6 copy.66
  165.1 18.2 %while.44 = (s32[]{:T(128)}, bf16[2,512,768]{2,1,0:T(8,128)(2,1)S(1)}, f32[2,12,512]{2,1,0:T(8,128)S(1)}, bf16[2,512,2304]{1,2,0:T(8,128)(2,1)}, s32[]{:T(128)}) while((s32[]{:T(128)}, bf16[2,512,768]{2,1,0:T(8,128)(2,1)S(1)}, f32[2,12,512]{2,1,0:T(8,128)S(1)}, bf16[2,512,2304]{1,2,0:T(8,128)(2,1)}, s32[]{:T(128)}) %tuple.124), condition=%wide.region_3.4_spmd, body=%wide.region_0.3_spmd.sunk | while | flops 834004992 | bytes 48996424 | solution.py:150
  195.5 36.3 %fusion.42 = (f32[1024,3072]{1,0:T(8,128)}, f32[1024,3072]{1,0:T(8,128)}) fusion(f32[3072]{0:T(1024)S(1)} %convert_element_type.210, bf16[1,768,3072]{2,1,0:T(8,128)(2,1)} %all-gather.25.cloned.1.call-done, f32[1024,768]{1,0:T(8,128)S(1)} %get-tuple-element.259, f32[768]{0:T(1024)S(1)} %get-tuple-element.177, f32[768]{0:T(1024)S(1)} %get-tuple-element.178, ...), kind=kOutput, calls=%fused_computation.78 | convolution fusion | flops 5033951232 | bytes 33056768 | tf_op jit(solution)/shard_map/dot_general | solution.py:28
  231.8 29.0 %all-gather.27.cloned.1.call-done = bf16[1,3072,768]{2,1,0:T(8,128)(2,1)} async-done(((bf16[1,96,768]{2,1,0:T(8,128)(2,1)}), bf16[1,3072,768]{2,1,0:T(8,128)(2,1)}) %all-gather.27.cloned.1.call-update) | async-done | bytes 4718608 | tf_op jit(solution)/shard_map/all_gather | solution.py:49
  260.8 12.7 %fusion.236 = (f32[1024]{0:T(1024)S(1)}, f32[1024,768]{1,0:T(8,128)S(1)}) fusion(f32[768]{0:T(1024)S(1)} %copy-done.73, bf16[1,3072,768]{2,1,0:T(8,128)(2,1)} %all-gather.27.cloned.1.call-done, f32[1024,3072]{1,0:T(8,128)} %get-tuple-element.260, f32[1024,3072]{1,0:T(8,128)} %get-tuple-element.261, f32[3072]{0:T(1024)S(1)} %convert_element_type.210, ...), kind=kOutput, calls=%fused_computation.320 | convolution fusion | flops 4849925120 | bytes 36209664 | tf_op jit(solution)/shard_map/dot_general | solution.py:28
  279.9 41.6 %all-gather.29.cloned.1.call-done = bf16[1,768,2304]{2,1,0:T(8,128)(2,1)} async-done(((bf16[1,24,2304]{2,1,0:T(8,128)(2,1)}), bf16[1,768,2304]{2,1,0:T(8,128)(2,1)}) %all-gather.29.cloned.1.call-update) | async-done | bytes 3538960 | tf_op jit(solution)/shard_map/all_gather | solution.py:45
  321.4 8.5 fusion.55
  330.0 6.7 copy.70
  336.8 18.5 %while.45 = (s32[]{:T(128)}, bf16[2,512,768]{2,1,0:T(8,128)(2,1)S(1)}, f32[2,12,512]{2,1,0:T(8,128)S(1)}, bf16[2,512,2304]{1,2,0:T(8,128)(2,1)}, s32[]{:T(128)}) while((s32[]{:T(128)}, bf16[2,512,768]{2,1,0:T(8,128)(2,1)S(1)}, f32[2,12,512]{2,1,0:T(8,128)S(1)}, bf16[2,512,2304]{1,2,0:T(8,128)(2,1)}, s32[]{:T(128)}) %tuple.127), condition=%wide.region_11.12_spmd, body=%wide.region_8.11_spmd.sunk | while | flops 834004992 | bytes 48996424 | solution.py:150
  355.3 22.0 %all-gather.31.cloned.1.call-done = bf16[1,768,768]{2,1,0:T(8,128)(2,1)} async-done(((bf16[1,24,768]{2,1,0:T(8,128)(2,1)}), bf16[1,768,768]{2,1,0:T(8,128)(2,1)}) %all-gather.31.cloned.1.call-update) | async-done | bytes 1179664 | tf_op jit(solution)/shard_map/all_gather | solution.py:46
  382.3 61.8 %all-gather.33.cloned.1.call-done = bf16[1,768,3072]{2,1,0:T(8,128)(2,1)} async-done(((bf16[1,24,3072]{2,1,0:T(8,128)(2,1)}), bf16[1,768,3072]{2,1,0:T(8,128)(2,1)}) %all-gather.33.cloned.1.call-update) | async-done | bytes 4718608 | tf_op jit(solution)/shard_map/all_gather | solution.py:47
  444.1 36.5 %fusion.43 = (f32[1024,3072]{1,0:T(8,128)}, f32[1024,3072]{1,0:T(8,128)}) fusion(f32[3072]{0:T(1024)S(1)} %copy-done.66, bf16[1,768,3072]{2,1,0:T(8,128)(2,1)} %all-gather.33.cloned.1.call-done, f32[1024,768]{1,0:T(8,128)S(1)} %get-tuple-element.265, f32[768]{0:T(1024)S(1)} %copy-done.71, f32[768]{0:T(1024)S(1)} %copy-done.69, f32[1024]{0:T(1024)S(1)} %fusion.214, ...), kind=kOutput, calls=%fused_computation.79 | convolution fusion | flops 5033951232 | bytes 33056768 | tf_op jit(solution)/shard_map/dot_general | solution.py:28
  480.6 28.8 %all-gather.35.cloned.1.call-done = bf16[1,3072,768]{2,1,0:T(8,128)(2,1)} async-done(((bf16[1,96,768]{2,1,0:T(8,128)(2,1)}), bf16[1,3072,768]{2,1,0:T(8,128)(2,1)}) %all-gather.35.cloned.1.call-update) | async-done | bytes 4718608 | tf_op jit(solution)/shard_map/all_gather | solution.py:49
  509.5 12.6 %fusion.238 = (f32[1024]{0:T(1024)S(1)}, f32[1024,768]{1,0:T(8,128)S(1)}) fusion(f32[768]{0:T(1024)S(1)} %copy-done.70, bf16[1,3072,768]{2,1,0:T(8,128)(2,1)} %all-gather.35.cloned.1.call-done, f32[1024,3072]{1,0:T(8,128)} %get-tuple-element.266, f32[1024,3072]{1,0:T(8,128)} %get-tuple-element.267, f32[3072]{0:T(1024)S(1)} %copy-done.66, ...), kind=kOutput, calls=%fused_computation.322 | convolution fusion | flops 4849925120 | bytes 36209664 | tf_op jit(solution)/shard_map/dot_general | solution.py:28
  526.4 22.2 %multiply_reduce_fusion.6 = (f32[1024]{0:T(1024)S(1)}, f32[1024,768]{1,0:T(8,128)}) fusion(f32[1024,768]{1,0:T(8,128)S(1)} %get-tuple-element.265, f32[1024]{0:T(1024)S(1)} %broadcast_multiply_fusion.1, f32[768]{0:T(1024)S(1)} %copy-done.69, bf16[1,768,3072]{2,1,0:T(8,128)(2,1)} %all-gather.33.cloned.1.call-done, f32[1024,3072]{1,0:T(8,128)} %get-tuple-element.266, ...), kind=kOutput, calls=%fused_computation.150 | convolution fusion | flops 9717152768 | bytes 44067840 | tf_op jit(solution)/shard_map/dot_general | solution.py:32
  558.2 83.9 %while.46 = (s32[]{:T(128)}, bf16[2,512,2304]{2,1,0:T(8,128)(2,1)}, bf16[2,512,2304]{1,2,0:T(8,128)(2,1)}, f32[2,12,512]{2,1,0:T(8,128)S(1)}, bf16[2,512,768]{2,1,0:T(8,128)(2,1)}, /*index=5*/s32[]{:T(128)}) while((s32[]{:T(128)}, bf16[2,512,2304]{2,1,0:T(8,128)(2,1)}, bf16[2,512,2304]{1,2,0:T(8,128)(2,1)}, f32[2,12,512]{2,1,0:T(8,128)S(1)}, ...), condition=%wide.region_22.23_spmd, body=%wide.region_20.22_spmd.sunk | while | flops 2055333888 | bytes 168870656 | solution.py:214
  569.9 11.5 %multiply_reduce_fusion.18 = (f32[12,512]{1,0:T(8,128)S(1)}, f32[12,512,512]{1,2,0:T(8,128)}) fusion(f32[12,512,512]{1,2,0:T(8,128)} %fusion.291, f32[12,512]{1,0:T(8,128)S(1)} %dynamic-slice_bitcast_fusion.4, bf16[512,12,64]{0,2,1:T(8,128)(2,1)S(1)} %bitcast.347, bf16[512,3,12,64]{0,3,2,1:T(8,128)(2,1)S(1)} %bitcast.338), kind=kOutput, calls=%fused_computation.29.clone.1 | convolution fusion | flops 415229952 | bytes 26796032 | tf_op jit(solution)/shard_map/while/body/eval_jaxpr/qhd,khd->hqk/dot_general | solution.py:97
  581.5 6.9 multiply_convert_fusion.16
  611.5 11.5 %multiply_reduce_fusion.18 = (f32[12,512]{1,0:T(8,128)S(1)}, f32[12,512,512]{1,2,0:T(8,128)}) fusion(f32[12,512,512]{1,2,0:T(8,128)} %fusion.291, f32[12,512]{1,0:T(8,128)S(1)} %dynamic-slice_bitcast_fusion.4, bf16[512,12,64]{0,2,1:T(8,128)(2,1)S(1)} %bitcast.347, bf16[512,3,12,64]{0,3,2,1:T(8,128)(2,1)S(1)} %bitcast.338), kind=kOutput, calls=%fused_computation.29.clone.1 | convolution fusion | flops 415229952 | bytes 26796032 | tf_op jit(solution)/shard_map/while/body/eval_jaxpr/qhd,khd->hqk/dot_general | solution.py:97
  623.1 6.9 multiply_convert_fusion.16
  659.8 21.1 %multiply_reduce_fusion.4 = (f32[1024]{0:T(1024)S(1)}, f32[1024,768]{1,0:T(8,128)}) fusion(f32[1024,768]{1,0:T(8,128)S(1)} %copy-done.7, f32[1024]{0:T(1024)S(1)} %copy-done.46, f32[768]{0:T(1024)S(1)} %copy-done.68, bf16[1,768,3072]{2,1,0:T(8,128)(2,1)} %all-gather.25.cloned.1.call-done, f32[1024,3072]{1,0:T(8,128)} %get-tuple-element.260, ...), kind=kOutput, calls=%fused_computation.146 | convolution fusion | flops 9717152768 | bytes 44067840 | tf_op jit(solution)/shard_map/dot_general | solution.py:32
  690.6 82.5 %while.47 = (s32[]{:T(128)}, bf16[2,512,2304]{2,1,0:T(8,128)(2,1)}, bf16[2,512,2304]{1,2,0:T(8,128)(2,1)}, f32[2,12,512]{2,1,0:T(8,128)S(1)}, bf16[2,512,768]{2,1,0:T(8,128)(2,1)}, /*index=5*/s32[]{:T(128)}) while((s32[]{:T(128)}, bf16[2,512,2304]{2,1,0:T(8,128)(2,1)}, bf16[2,512,2304]{1,2,0:T(8,128)(2,1)}, f32[2,12,512]{2,1,0:T(8,128)S(1)}, ...), condition=%wide.region_29.30_spmd, body=%wide.region_27.29_spmd.sunk | while | flops 2055333888 | bytes 168477376 | solution.py:214
  701.4 11.5 %multiply_reduce_fusion.19 = (f32[12,512]{1,0:T(8,128)S(1)}, f32[12,512,512]{1,2,0:T(8,128)}) fusion(f32[12,512,512]{1,2,0:T(8,128)} %fusion.300, f32[12,512]{1,0:T(8,128)S(1)} %dynamic-slice_bitcast_fusion.5, bf16[512,12,64]{0,2,1:T(8,128)(2,1)S(1)} %bitcast.349, bf16[512,3,12,64]{0,3,2,1:T(8,128)(2,1)S(1)} %bitcast.342), kind=kOutput, calls=%fused_computation.53.clone.1 | convolution fusion | flops 415229952 | bytes 26796032 | tf_op jit(solution)/shard_map/while/body/eval_jaxpr/qhd,khd->hqk/dot_general | solution.py:97
  713.4 6.9 multiply_convert_fusion.17
  742.5 11.5 %multiply_reduce_fusion.19 = (f32[12,512]{1,0:T(8,128)S(1)}, f32[12,512,512]{1,2,0:T(8,128)}) fusion(f32[12,512,512]{1,2,0:T(8,128)} %fusion.300, f32[12,512]{1,0:T(8,128)S(1)} %dynamic-slice_bitcast_fusion.5, bf16[512,12,64]{0,2,1:T(8,128)(2,1)S(1)} %bitcast.349, bf16[512,3,12,64]{0,3,2,1:T(8,128)(2,1)S(1)} %bitcast.342), kind=kOutput, calls=%fused_computation.53.clone.1 | convolution fusion | flops 415229952 | bytes 26796032 | tf_op jit(solution)/shard_map/while/body/eval_jaxpr/qhd,khd->hqk/dot_general | solution.py:97
  754.6 6.9 multiply_convert_fusion.17
  781.7 6.9 fusion.87
  791.3 112.9 %all-reduce.6.cloned.1.call-done = (f32[1,8,768]{2,1,0:T(8,128)}, f32[1,8,768]{2,1,0:T(8,128)}, f32[1,8,768]{2,1,0:T(8,128)}, f32[1,8,768]{2,1,0:T(8,128)}) async-done(((f32[1,8,768]{2,1,0:T(8,128)}, f32[1,8,768]{2,1,0:T(8,128)}, f32[1,8,768]{2,1,0:T(8,128)}, f32[1,8,768]{2,1,0:T(8,128)}), (f32[1,8,768]{2,1,0:T(8,128)}, f32[1,8,768]{2,1,0:T(8,128)}, f32[1,8,768]{2,1,0:T(8,128)}, ...) | async-done | bytes 98320 | tf_op jit(solution)/shard_map/psum | solution.py:309
  (361 shorter events, 227.0 us)
Async XLA Ops:
  7.2 138.8 %copy-start = (bf16[2,80,768]{2,1,0:T(8,128)(2,1)S(1)}, bf16[2,80,768]{2,1,0:T(8,128)(2,1)}, u32[]{:S(2)}) copy-start(bf16[2,80,768]{2,1,0:T(8,128)(2,1)} %param.21) | copy-start | bytes 737284
  7.2 141.8 %all-gather.21.cloned.1.call-start = ((), (), s32[]{:S(2)}) async-start(), calls=%async_computation | async-start | bytes 3649536 | tf_op jit(solution)/shard_map/all_gather | solution.py:45
  9.0 174.5 %all-gather.23.cloned.1.call-start = ((), (), s32[]{:S(2)}) async-start(), calls=%async_computation.1 | async-start | bytes 1216512 | tf_op jit(solution)/shard_map/all_gather | solution.py:46
  10.5 185.0 %all-gather.25.cloned.1.call-start = ((), (), s32[]{:S(2)}) async-start(), calls=%async_computation.2 | async-start | bytes 4866048 | tf_op jit(solution)/shard_map/all_gather | solution.py:47
  12.3 83.3 %copy-start.40 = (f32[2,8,768]{2,1,0:T(8,128)S(1)}, f32[2,8,768]{2,1,0:T(8,128)}, u32[]{:S(2)}) copy-start(f32[2,8,768]{2,1,0:T(8,128)} %param.31) | copy-start | bytes 147460
  12.3 83.3 %copy-start.41 = (f32[2,8,768]{2,1,0:T(8,128)S(1)}, f32[2,8,768]{2,1,0:T(8,128)}, u32[]{:S(2)}) copy-start(f32[2,8,768]{2,1,0:T(8,128)} %param.30) | copy-start | bytes 147460
  12.3 83.4 %copy-start.19 = (bf16[2,512,768]{2,1,0:T(8,128)(2,1)S(1)}, bf16[2,512,768]{2,1,0:T(8,128)(2,1)}, u32[]{:S(2)}) copy-start(bf16[2,512,768]{2,1,0:T(8,128)(2,1)} %param.20) | copy-start | bytes 4718596
  12.3 248.5 %all-gather.27.cloned.1.call-start = ((), (), s32[]{:S(2)}) async-start(), calls=%async_computation.3 | async-start | bytes 4866048 | tf_op jit(solution)/shard_map/all_gather | solution.py:49
  14.2 307.2 %all-gather.29.cloned.1.call-start = ((), (), s32[]{:S(2)}) async-start(), calls=%async_computation.4 | async-start | bytes 3649536 | tf_op jit(solution)/shard_map/all_gather | solution.py:45
  14.8 362.4 %all-gather.31.cloned.1.call-start = ((), (), s32[]{:S(2)}) async-start(), calls=%async_computation.5 | async-start | bytes 1216512 | tf_op jit(solution)/shard_map/all_gather | solution.py:46
  15.4 428.7 %all-gather.33.cloned.1.call-start = ((), (), s32[]{:S(2)}) async-start(), calls=%async_computation.6 | async-start | bytes 4866048 | tf_op jit(solution)/shard_map/all_gather | solution.py:47
  16.1 493.4 %all-gather.35.cloned.1.call-start = ((), (), s32[]{:S(2)}) async-start(), calls=%async_computation.7 | async-start | bytes 4866048 | tf_op jit(solution)/shard_map/all_gather | solution.py:49
  16.9 887.4 %all-reduce.6.cloned.1.call-start = ((), (), s32[]{:S(2)}) async-start(), calls=%async_computation.8 | async-start | bytes 196608 | tf_op jit(solution)/shard_map/psum | solution.py:309
  95.5 165.2 %copy-start.67 = (f32[768]{0:T(1024)}, f32[768]{0:T(1024)S(1)}, u32[]{:S(2)}) copy-start(f32[768]{0:T(1024)S(1)} %get-tuple-element.178) | copy-start | bytes 9220
  95.5 50.4 %copy-start.75 = (s32[2,80]{1,0:T(2,128)S(1)}, s32[2,80]{1,0:T(2,128)}, u32[]{:S(2)}) copy-start(s32[2,80]{1,0:T(2,128)} %param.22) | copy-start | bytes 1924
  145.3 115.5 %copy-start.64 = (f32[3072]{0:T(1024)}, f32[3072]{0:T(1024)S(1)}, u32[]{:S(2)}) copy-start(f32[3072]{0:T(1024)S(1)} %convert_element_type.210) | copy-start | bytes 36868
  188.3 72.4 %copy-start.6 = (f32[1024,768]{1,0:T(8,128)}, f32[1024,768]{1,0:T(8,128)S(1)}, u32[]{:S(2)}) copy-start(f32[1024,768]{1,0:T(8,128)S(1)} %get-tuple-element.259) | copy-start | bytes 9437188
  188.3 72.4 %copy-start.45 = (f32[1024]{0:T(1024)}, f32[1024]{0:T(1024)S(1)}, u32[]{:S(2)}) copy-start(f32[1024]{0:T(1024)S(1)} %broadcast_multiply_fusion.3) | copy-start | bytes 12292
  188.9 71.9 %copy-start.55 = (f32[1024]{0:T(1024)}, f32[1024]{0:T(1024)S(1)}, u32[]{:S(2)}) copy-start(f32[1024]{0:T(1024)S(1)} %fusion.212) | copy-start | bytes 12292
  195.5 65.3 %copy-start.73 = (f32[768]{0:T(1024)S(1)}, f32[768]{0:T(1024)}, u32[]{:S(2)}) copy-start(f32[768]{0:T(1024)} %get-tuple-element.176) | copy-start | bytes 9220
  273.6 103.7 %copy-start.30 = (f32[1024]{0:T(1024)}, f32[1024]{0:T(1024)S(1)}, u32[]{:S(2)}) copy-start(f32[1024]{0:T(1024)S(1)} %broadcast_multiply_fusion.2) | copy-start | bytes 12292
  274.1 103.2 %copy-start.47 = (f32[1024]{0:T(1024)}, f32[1024]{0:T(1024)S(1)}, u32[]{:S(2)}) copy-start(f32[1024]{0:T(1024)S(1)} %fusion.213) | copy-start | bytes 12292
  275.3 54.7 %copy-start.28 = (bf16[1024,16]{0,1:T(8,128)(2,1)}, bf16[1024,16]{0,1:T(8,128)(2,1)S(1)}, u32[]{:S(2)}) copy-start(bf16[1024,16]{0,1:T(8,128)(2,1)S(1)} %convolution_convert_fusion.2) | copy-start | bytes 98308
  377.2 66.8 %copy-start.66 = (f32[3072]{0:T(1024)S(1)}, f32[3072]{0:T(1024)}, u32[]{:S(2)}) copy-start(f32[3072]{0:T(1024)} %convert_element_type.211) | copy-start | bytes 36868
  377.2 66.8 %copy-start.69 = (f32[768]{0:T(1024)S(1)}, f32[768]{0:T(1024)}, u32[]{:S(2)}) copy-start(f32[768]{0:T(1024)} %get-tuple-element.170) | copy-start | bytes 9220
  377.3 66.8 %copy-start.71 = (f32[768]{0:T(1024)S(1)}, f32[768]{0:T(1024)}, u32[]{:S(2)}) copy-start(f32[768]{0:T(1024)} %get-tuple-element.169) | copy-start | bytes 9220
  444.1 65.4 %copy-start.70 = (f32[768]{0:T(1024)S(1)}, f32[768]{0:T(1024)}, u32[]{:S(2)}) copy-start(f32[768]{0:T(1024)} %get-tuple-element.168) | copy-start | bytes 9220
  558.2 83.9 %copy-start.29 = (bf16[1024,16]{0,1:T(8,128)(2,1)S(1)}, bf16[1024,16]{0,1:T(8,128)(2,1)}, u32[]{:S(2)}) copy-start(bf16[1024,16]{0,1:T(8,128)(2,1)} %copy-done.28) | copy-start | bytes 98308
  558.2 88.7 %copy-start.34 = (bf16[2,8,768]{2,1,0:T(8,128)(2,1)S(1)}, bf16[2,8,768]{2,1,0:T(8,128)(2,1)}, u32[]{:S(2)}) copy-start(bf16[2,8,768]{2,1,0:T(8,128)(2,1)} %copy-done.32) | copy-start | bytes 73732
  690.6 82.5 %copy-start.27 = (bf16[1024,16]{0,1:T(8,128)(2,1)S(1)}, bf16[1024,16]{0,1:T(8,128)(2,1)}, u32[]{:S(2)}) copy-start(bf16[1024,16]{0,1:T(8,128)(2,1)} %copy-done.26) | copy-start | bytes 98308
  690.6 87.2 %copy-start.39 = (bf16[2,8,768]{2,1,0:T(8,128)(2,1)S(1)}, bf16[2,8,768]{2,1,0:T(8,128)(2,1)}, u32[]{:S(2)}) copy-start(bf16[2,8,768]{2,1,0:T(8,128)(2,1)} %copy-done.36) | copy-start | bytes 73732
  781.7 124.0 %copy-start.1 = (bf16[2,80,768]{2,1,0:T(8,128)(2,1)S(1)}, bf16[2,80,768]{2,1,0:T(8,128)(2,1)}, u32[]{:S(2)}) copy-start(bf16[2,80,768]{2,1,0:T(8,128)(2,1)} %param.21) | copy-start | bytes 737284
  (72 other events, 706.1 us)
Sparse Core Ops, SparseCore 0:
  11.5 61.4 all-gather.20
  76.4 52.3 all-gather.22
  131.8 63.6 all-gather.24
  198.2 62.4 all-gather.26
  263.5 57.9 all-gather.28
  324.8 52.4 all-gather.30
  380.1 63.9 all-gather.32
  447.0 62.4 all-gather.34
  781.8 122.4 all-reduce.5
where the time goes:
time: 919 us; the launch traced here: 912 us
  matrix products  329 us (36%)
  waiting for transfers between devices  305 us (33%)
  blocking collectives  119 us (13%)
  local copies, waits for them, and re-layouts  87.3 us (9%)
  other arithmetic  53.9 us (6%)
  between operations  15 us (2%)
    dot_general x14, matrix products, matrix_multiply(): return jnp.dot(left, right, preferred_element_type=jnp.float32)  133 us
    psum x1, waiting for transfers between devices, on_device(): lax.psum((query_gradient_total, value_gradient_total), ('dp', 'fsdp'))  113 us
    all_gather x2, blocking collectives, fetch_forward(): lax.all_gather(layer_small, ('dp', 'fsdp'), axis=0, tiled=True)  73.5 us
    dot_general x12, matrix products, transposed_multiply(): lax.dot_general(left, right, (((1,), (1,)), ((), ())), preferred_element_...  72.1 us
    all_gather x2, waiting for transfers between devices, fetch_forward(): lax.all_gather(layer_in, ('dp', 'fsdp'), axis=0, tiled=True)  68.4 us
    all_gather x2, waiting for transfers between devices, fetch_forward(): lax.all_gather(layer_out, ('dp', 'fsdp'), axis=0, tiled=True)  57.8 us
    dot_general x4, matrix products, attend_back(): jnp.einsum('qhd,khd->hqk', grad_view, value_matrix_rows, preferred_elemen...  46.1 us
    unnamed x1, blocking collectives  45.6 us
  transfers between devices with their start and end apart: 9, of which 7 were waited for; matrix products, arithmetic and copies ran while one was open for 21% of the time, Pallas kernels for 0%

commit v1 on v0

--- a/solution.py
+++ b/solution.py
@@ -307,7 +307,7 @@
             value_up_weight[layer_index],
         )
         query_gradient_total, value_gradient_total = lax.psum(
-            (query_gradient_total, value_gradient_total), ("dp", "fsdp")
+            lax.psum((query_gradient_total, value_gradient_total), "fsdp"), "dp"
         )
         query_gradient_stack[layer_index] = query_gradient_total
         value_gradient_stack[layer_index] = value_gradient_total

time: 919 us -> 924 us (level)
    psum x1 -> x2, waiting for transfers between devices: 113 us -> 112 us  [the longest x1 107 us: on_device(): lax.psum(lax.psum((query_gradient_total, value_gradient_total), 'fsdp'),...]
  transfers between devices with their start and end apart: 9 -> 10, of which waited for: 7 -> 8; matrix products, arithmetic and copies ran while one was open for 21% -> 22% of each run, Pallas kernels for 0% -> 0%
where the time goes in v1:
time: 924 us; the launch traced here: 916 us
  matrix products  333 us (36%)
  waiting for transfers between devices  305 us (33%)
  blocking collectives  119 us (13%)
  local copies, waits for them, and re-layouts  86.9 us (9%)
  other arithmetic  54 us (6%)
  between operations  15.3 us (2%)
    dot_general x14, matrix products, matrix_multiply(): return jnp.dot(left, right, preferred_element_type=jnp.float32)  133 us
    psum x1, waiting for transfers between devices, on_device(): lax.psum(lax.psum((query_gradient_total, value_gradient_total), 'fsdp'),...  107 us
    dot_general x12, matrix products, transposed_multiply(): lax.dot_general(left, right, (((1,), (1,)), ((), ())), preferred_element_...  76 us
    all_gather x2, blocking collectives, fetch_forward(): lax.all_gather(layer_small, ('dp', 'fsdp'), axis=0, tiled=True)  73.5 us
    all_gather x2, waiting for transfers between devices, fetch_forward(): lax.all_gather(layer_in, ('dp', 'fsdp'), axis=0, tiled=True)  68.5 us
    all_gather x2, waiting for transfers between devices, fetch_forward(): lax.all_gather(layer_out, ('dp', 'fsdp'), axis=0, tiled=True)  57.9 us
    dot_general x4, matrix products, attend_back(): jnp.einsum('qhd,khd->hqk', grad_view, value_matrix_rows, preferred_elemen...  46 us
    unnamed x1, blocking collectives  45.4 us
  transfers between devices with their start and end apart: 10, of which 8 were waited for; matrix products, arithmetic and copies ran while one was open for 22% of the time, Pallas kernels for 0%

profile of v1, /device:TPU:8, one launch (start us, length us, event | category | flops | bytes accessed | tf_op | source)
XLA Modules:
  0.0 916.0 jit_solution(5538297534358250238)
XLA Ops:
  17.6 36.0 %all-gather.7 = bf16[1,768,24]{2,1,0:T(8,128)(2,1)S(1)} all-gather(bf16[1,24,24]{2,1,0:T(8,128)(2,1)S(1)} %get-tuple-element.253), channel_id=9, replica_groups=mesh['dp'=16,'fsdp'=2] {'dp','fsdp'}, dimensions={1}, use_global_device_ids=true | all-gather | bytes 38016 | tf_op jit(solution)/shard_map/all_gather | solution.py:50
  56.4 37.5 %all-gather.1 = bf16[1,768,24]{2,1,0:T(8,128)(2,1)S(1)} all-gather(bf16[1,24,24]{2,1,0:T(8,128)(2,1)S(1)} %get-tuple-element.254), channel_id=3, replica_groups=mesh['dp'=16,'fsdp'=2] {'dp','fsdp'}, dimensions={1}, use_global_device_ids=true | all-gather | bytes 38016 | tf_op jit(solution)/shard_map/all_gather | solution.py:50
  99.7 45.4 %all-reduce.4 = (bf16[3072]{0:T(1024)(128)(2,1)S(1)}, bf16[3072]{0:T(1024)(128)(2,1)S(1)}) all-reduce(bf16[3072]{0:T(1024)(128)(2,1)S(1)} %dynamic-update-slice, bf16[3072]{0:T(1024)(128)(2,1)S(1)} %dynamic-update-slice.1), channel_id=6, replica_groups=mesh['dp'=16,'fsdp'=2] {'dp','fsdp'}, use_global_device_ids=true, to_apply=%add | all-reduce | flops 6144 | bytes 24576
  148.9 9.4 %fusion.54 = bf16[1024,2304]{1,0:T(8,128)(2,1)} fusion(f32[1024,768]{1,0:T(8,128)S(1)} %convolution_multiply_fusion.2, f32[1024,768]{1,0:T(8,128)} %convolution_multiply_fusion.3, bf16[1024,768]{1,0:T(8,128)(2,1)} %bitcast.373, f32[2304]{0:T(1024)S(1)} %get-tuple-element.259, f32[2304]{0:T(1024)S(1)} %get-tuple-element.258, ...), kind=kOutput, calls=%fused_computation.111 | convolution fusion | flops 3635675136 | bytes 16140288 | tf_op jit(solution)/shard_map/dot_general | solution.py:28
  165.1 18.2 %while.44 = (s32[]{:T(128)}, bf16[2,512,768]{2,1,0:T(8,128)(2,1)S(1)}, f32[2,12,512]{2,1,0:T(8,128)S(1)}, bf16[2,512,2304]{1,2,0:T(8,128)(2,1)}, s32[]{:T(128)}) while((s32[]{:T(128)}, bf16[2,512,768]{2,1,0:T(8,128)(2,1)S(1)}, f32[2,12,512]{2,1,0:T(8,128)S(1)}, bf16[2,512,2304]{1,2,0:T(8,128)(2,1)}, s32[]{:T(128)}) %tuple.124), condition=%wide.region_3.4_spmd, body=%wide.region_0.3_spmd.sunk | while | flops 834004992 | bytes 48996424 | solution.py:150
  188.8 6.7 all-gather.25.cloned.1.call-done
  195.5 36.2 %fusion.42 = (f32[1024,3072]{1,0:T(8,128)}, f32[1024,3072]{1,0:T(8,128)}) fusion(f32[3072]{0:T(1024)S(1)} %convert_element_type.210, bf16[1,768,3072]{2,1,0:T(8,128)(2,1)} %all-gather.25.cloned.1.call-done, f32[1024,768]{1,0:T(8,128)S(1)} %get-tuple-element.263, f32[768]{0:T(1024)S(1)} %get-tuple-element.177, f32[768]{0:T(1024)S(1)} %get-tuple-element.178, ...), kind=kOutput, calls=%fused_computation.78 | convolution fusion | flops 5033951232 | bytes 33056768 | tf_op jit(solution)/shard_map/dot_general | solution.py:28
  231.8 29.0 %all-gather.27.cloned.1.call-done = bf16[1,3072,768]{2,1,0:T(8,128)(2,1)} async-done(((bf16[1,96,768]{2,1,0:T(8,128)(2,1)}), bf16[1,3072,768]{2,1,0:T(8,128)(2,1)}) %all-gather.27.cloned.1.call-update) | async-done | bytes 4718608 | tf_op jit(solution)/shard_map/all_gather | solution.py:49
  260.8 12.7 %fusion.224 = (f32[1024]{0:T(1024)S(1)}, f32[1024,768]{1,0:T(8,128)S(1)}) fusion(f32[768]{0:T(1024)S(1)} %copy-done.72, bf16[1,3072,768]{2,1,0:T(8,128)(2,1)} %all-gather.27.cloned.1.call-done, f32[1024,3072]{1,0:T(8,128)} %get-tuple-element.264, f32[1024,3072]{1,0:T(8,128)} %get-tuple-element.265, f32[3072]{0:T(1024)S(1)} %convert_element_type.210, ...), kind=kOutput, calls=%fused_computation.316 | convolution fusion | flops 4849925120 | bytes 36209664 | tf_op jit(solution)/shard_map/dot_general | solution.py:28
  279.9 41.6 %all-gather.29.cloned.1.call-done = bf16[1,768,2304]{2,1,0:T(8,128)(2,1)} async-done(((bf16[1,24,2304]{2,1,0:T(8,128)(2,1)}), bf16[1,768,2304]{2,1,0:T(8,128)(2,1)}) %all-gather.29.cloned.1.call-update) | async-done | bytes 3538960 | tf_op jit(solution)/shard_map/all_gather | solution.py:45
  321.5 8.5 fusion.55
  330.0 6.7 copy.70
  336.8 18.5 %while.45 = (s32[]{:T(128)}, bf16[2,512,768]{2,1,0:T(8,128)(2,1)S(1)}, f32[2,12,512]{2,1,0:T(8,128)S(1)}, bf16[2,512,2304]{1,2,0:T(8,128)(2,1)}, s32[]{:T(128)}) while((s32[]{:T(128)}, bf16[2,512,768]{2,1,0:T(8,128)(2,1)S(1)}, f32[2,12,512]{2,1,0:T(8,128)S(1)}, bf16[2,512,2304]{1,2,0:T(8,128)(2,1)}, s32[]{:T(128)}) %tuple.127), condition=%wide.region_11.12_spmd, body=%wide.region_8.11_spmd.sunk | while | flops 834004992 | bytes 48996424 | solution.py:150
  355.3 22.0 %all-gather.31.cloned.1.call-done = bf16[1,768,768]{2,1,0:T(8,128)(2,1)} async-done(((bf16[1,24,768]{2,1,0:T(8,128)(2,1)}), bf16[1,768,768]{2,1,0:T(8,128)(2,1)}) %all-gather.31.cloned.1.call-update) | async-done | bytes 1179664 | tf_op jit(solution)/shard_map/all_gather | solution.py:46
  382.3 61.8 %all-gather.33.cloned.1.call-done = bf16[1,768,3072]{2,1,0:T(8,128)(2,1)} async-done(((bf16[1,24,3072]{2,1,0:T(8,128)(2,1)}), bf16[1,768,3072]{2,1,0:T(8,128)(2,1)}) %all-gather.33.cloned.1.call-update) | async-done | bytes 4718608 | tf_op jit(solution)/shard_map/all_gather | solution.py:47
  444.1 36.5 %fusion.43 = (f32[1024,3072]{1,0:T(8,128)}, f32[1024,3072]{1,0:T(8,128)}) fusion(f32[3072]{0:T(1024)S(1)} %copy-done.65, bf16[1,768,3072]{2,1,0:T(8,128)(2,1)} %all-gather.33.cloned.1.call-done, f32[1024,768]{1,0:T(8,128)S(1)} %get-tuple-element.269, f32[768]{0:T(1024)S(1)} %copy-done.70, f32[768]{0:T(1024)S(1)} %copy-done.68, f32[1024]{0:T(1024)S(1)} %fusion.202, ...), kind=kOutput, calls=%fused_computation.79 | convolution fusion | flops 5033951232 | bytes 33056768 | tf_op jit(solution)/shard_map/dot_general | solution.py:28
  480.7 28.9 %all-gather.35.cloned.1.call-done = bf16[1,3072,768]{2,1,0:T(8,128)(2,1)} async-done(((bf16[1,96,768]{2,1,0:T(8,128)(2,1)}), bf16[1,3072,768]{2,1,0:T(8,128)(2,1)}) %all-gather.35.cloned.1.call-update) | async-done | bytes 4718608 | tf_op jit(solution)/shard_map/all_gather | solution.py:49
  509.5 12.6 %fusion.226 = (f32[1024]{0:T(1024)S(1)}, f32[1024,768]{1,0:T(8,128)S(1)}) fusion(f32[768]{0:T(1024)S(1)} %copy-done.69, bf16[1,3072,768]{2,1,0:T(8,128)(2,1)} %all-gather.35.cloned.1.call-done, f32[1024,3072]{1,0:T(8,128)} %get-tuple-element.270, f32[1024,3072]{1,0:T(8,128)} %get-tuple-element.271, f32[3072]{0:T(1024)S(1)} %copy-done.65, ...), kind=kOutput, calls=%fused_computation.318 | convolution fusion | flops 4849925120 | bytes 36209664 | tf_op jit(solution)/shard_map/dot_general | solution.py:28
  526.4 22.2 %multiply_reduce_fusion.6 = (f32[1024]{0:T(1024)S(1)}, f32[1024,768]{1,0:T(8,128)}) fusion(f32[1024,768]{1,0:T(8,128)S(1)} %get-tuple-element.269, f32[1024]{0:T(1024)S(1)} %broadcast_multiply_fusion.1, f32[768]{0:T(1024)S(1)} %copy-done.68, bf16[1,768,3072]{2,1,0:T(8,128)(2,1)} %all-gather.33.cloned.1.call-done, f32[1024,3072]{1,0:T(8,128)} %get-tuple-element.270, ...), kind=kOutput, calls=%fused_computation.150 | convolution fusion | flops 9717152768 | bytes 44067840 | tf_op jit(solution)/shard_map/dot_general | solution.py:32
  558.2 83.9 %while.46 = (s32[]{:T(128)}, bf16[2,512,2304]{2,1,0:T(8,128)(2,1)}, bf16[2,512,2304]{1,2,0:T(8,128)(2,1)}, f32[2,12,512]{2,1,0:T(8,128)S(1)}, bf16[2,512,768]{2,1,0:T(8,128)(2,1)}, /*index=5*/s32[]{:T(128)}) while((s32[]{:T(128)}, bf16[2,512,2304]{2,1,0:T(8,128)(2,1)}, bf16[2,512,2304]{1,2,0:T(8,128)(2,1)}, f32[2,12,512]{2,1,0:T(8,128)S(1)}, ...), condition=%wide.region_22.23_spmd, body=%wide.region_20.22_spmd.sunk | while | flops 2055333888 | bytes 168870656 | solution.py:214
  569.9 11.5 %multiply_reduce_fusion.18 = (f32[12,512]{1,0:T(8,128)S(1)}, f32[12,512,512]{1,2,0:T(8,128)}) fusion(f32[12,512,512]{1,2,0:T(8,128)} %fusion.279, f32[12,512]{1,0:T(8,128)S(1)} %dynamic-slice_bitcast_fusion.4, bf16[512,12,64]{0,2,1:T(8,128)(2,1)S(1)} %bitcast.343, bf16[512,3,12,64]{0,3,2,1:T(8,128)(2,1)S(1)} %bitcast.334), kind=kOutput, calls=%fused_computation.29.clone.1 | convolution fusion | flops 415229952 | bytes 26796032 | tf_op jit(solution)/shard_map/while/body/eval_jaxpr/qhd,khd->hqk/dot_general | solution.py:97
  581.5 6.9 multiply_convert_fusion.16
  611.5 11.5 %multiply_reduce_fusion.18 = (f32[12,512]{1,0:T(8,128)S(1)}, f32[12,512,512]{1,2,0:T(8,128)}) fusion(f32[12,512,512]{1,2,0:T(8,128)} %fusion.279, f32[12,512]{1,0:T(8,128)S(1)} %dynamic-slice_bitcast_fusion.4, bf16[512,12,64]{0,2,1:T(8,128)(2,1)S(1)} %bitcast.343, bf16[512,3,12,64]{0,3,2,1:T(8,128)(2,1)S(1)} %bitcast.334), kind=kOutput, calls=%fused_computation.29.clone.1 | convolution fusion | flops 415229952 | bytes 26796032 | tf_op jit(solution)/shard_map/while/body/eval_jaxpr/qhd,khd->hqk/dot_general | solution.py:97
  623.1 6.9 multiply_convert_fusion.16
  659.8 21.1 %multiply_reduce_fusion.4 = (f32[1024]{0:T(1024)S(1)}, f32[1024,768]{1,0:T(8,128)}) fusion(f32[1024,768]{1,0:T(8,128)S(1)} %copy-done.7, f32[1024]{0:T(1024)S(1)} %copy-done.45, f32[768]{0:T(1024)S(1)} %copy-done.67, bf16[1,768,3072]{2,1,0:T(8,128)(2,1)} %all-gather.25.cloned.1.call-done, f32[1024,3072]{1,0:T(8,128)} %get-tuple-element.264, ...), kind=kOutput, calls=%fused_computation.146 | convolution fusion | flops 9717152768 | bytes 44067840 | tf_op jit(solution)/shard_map/dot_general | solution.py:32
  690.5 82.1 %while.47 = (s32[]{:T(128)}, bf16[2,512,2304]{2,1,0:T(8,128)(2,1)}, bf16[2,512,2304]{1,2,0:T(8,128)(2,1)}, f32[2,12,512]{2,1,0:T(8,128)S(1)}, bf16[2,512,768]{2,1,0:T(8,128)(2,1)}, /*index=5*/s32[]{:T(128)}) while((s32[]{:T(128)}, bf16[2,512,2304]{2,1,0:T(8,128)(2,1)}, bf16[2,512,2304]{1,2,0:T(8,128)(2,1)}, f32[2,12,512]{2,1,0:T(8,128)S(1)}, ...), condition=%wide.region_29.30_spmd, body=%wide.region_27.29_spmd.sunk | while | flops 2055333888 | bytes 168477376 | solution.py:214
  701.2 11.5 %multiply_reduce_fusion.19 = (f32[12,512]{1,0:T(8,128)S(1)}, f32[12,512,512]{1,2,0:T(8,128)}) fusion(f32[12,512,512]{1,2,0:T(8,128)} %fusion.288, f32[12,512]{1,0:T(8,128)S(1)} %dynamic-slice_bitcast_fusion.5, bf16[512,12,64]{0,2,1:T(8,128)(2,1)S(1)} %bitcast.345, bf16[512,3,12,64]{0,3,2,1:T(8,128)(2,1)S(1)} %bitcast.338), kind=kOutput, calls=%fused_computation.53.clone.1 | convolution fusion | flops 415229952 | bytes 26796032 | tf_op jit(solution)/shard_map/while/body/eval_jaxpr/qhd,khd->hqk/dot_general | solution.py:97
  713.2 6.9 multiply_convert_fusion.17
  742.2 11.5 %multiply_reduce_fusion.19 = (f32[12,512]{1,0:T(8,128)S(1)}, f32[12,512,512]{1,2,0:T(8,128)}) fusion(f32[12,512,512]{1,2,0:T(8,128)} %fusion.288, f32[12,512]{1,0:T(8,128)S(1)} %dynamic-slice_bitcast_fusion.5, bf16[512,12,64]{0,2,1:T(8,128)(2,1)S(1)} %bitcast.345, bf16[512,3,12,64]{0,3,2,1:T(8,128)(2,1)S(1)} %bitcast.338), kind=kOutput, calls=%fused_computation.53.clone.1 | convolution fusion | flops 415229952 | bytes 26796032 | tf_op jit(solution)/shard_map/while/body/eval_jaxpr/qhd,khd->hqk/dot_general | solution.py:97
  754.1 6.9 multiply_convert_fusion.17
  779.5 9.1 fusion.87
  800.7 106.9 %all-reduce.8.cloned.1.call-done = (f32[1,8,768]{2,1,0:T(8,128)}, f32[1,8,768]{2,1,0:T(8,128)}, f32[1,8,768]{2,1,0:T(8,128)}, f32[1,8,768]{2,1,0:T(8,128)}) async-done(((f32[1,8,768]{2,1,0:T(8,128)}, f32[1,8,768]{2,1,0:T(8,128)}, f32[1,8,768]{2,1,0:T(8,128)}, f32[1,8,768]{2,1,0:T(8,128)}), (f32[1,8,768]{2,1,0:T(8,128)}, f32[1,8,768]{2,1,0:T(8,128)}, f32[1,8,768]{2,1,0:T(8,128)}, ...) | async-done | bytes 98320 | tf_op jit(solution)/shard_map/psum | solution.py:309
  (362 shorter events, 234.3 us)
Async XLA Ops:
  7.2 138.7 %copy-start = (bf16[2,80,768]{2,1,0:T(8,128)(2,1)S(1)}, bf16[2,80,768]{2,1,0:T(8,128)(2,1)}, u32[]{:S(2)}) copy-start(bf16[2,80,768]{2,1,0:T(8,128)(2,1)} %param.21) | copy-start | bytes 737284
  7.2 141.7 %all-gather.21.cloned.1.call-start = ((), (), s32[]{:S(2)}) async-start(), calls=%async_computation | async-start | bytes 3649536 | tf_op jit(solution)/shard_map/all_gather | solution.py:45
  9.0 174.4 %all-gather.23.cloned.1.call-start = ((), (), s32[]{:S(2)}) async-start(), calls=%async_computation.1 | async-start | bytes 1216512 | tf_op jit(solution)/shard_map/all_gather | solution.py:46
  10.5 185.1 %all-gather.25.cloned.1.call-start = ((), (), s32[]{:S(2)}) async-start(), calls=%async_computation.2 | async-start | bytes 4866048 | tf_op jit(solution)/shard_map/all_gather | solution.py:47
  12.3 83.4 %copy-start.39 = (f32[2,8,768]{2,1,0:T(8,128)S(1)}, f32[2,8,768]{2,1,0:T(8,128)}, u32[]{:S(2)}) copy-start(f32[2,8,768]{2,1,0:T(8,128)} %param.31) | copy-start | bytes 147460
  12.3 83.4 %copy-start.40 = (f32[2,8,768]{2,1,0:T(8,128)S(1)}, f32[2,8,768]{2,1,0:T(8,128)}, u32[]{:S(2)}) copy-start(f32[2,8,768]{2,1,0:T(8,128)} %param.30) | copy-start | bytes 147460
  12.3 83.4 %copy-start.18 = (bf16[2,512,768]{2,1,0:T(8,128)(2,1)S(1)}, bf16[2,512,768]{2,1,0:T(8,128)(2,1)}, u32[]{:S(2)}) copy-start(bf16[2,512,768]{2,1,0:T(8,128)(2,1)} %param.20) | copy-start | bytes 4718596
  12.3 248.5 %all-gather.27.cloned.1.call-start = ((), (), s32[]{:S(2)}) async-start(), calls=%async_computation.3 | async-start | bytes 4866048 | tf_op jit(solution)/shard_map/all_gather | solution.py:49
  14.2 307.3 %all-gather.29.cloned.1.call-start = ((), (), s32[]{:S(2)}) async-start(), calls=%async_computation.4 | async-start | bytes 3649536 | tf_op jit(solution)/shard_map/all_gather | solution.py:45
  14.8 362.5 %all-gather.31.cloned.1.call-start = ((), (), s32[]{:S(2)}) async-start(), calls=%async_computation.5 | async-start | bytes 1216512 | tf_op jit(solution)/shard_map/all_gather | solution.py:46
  15.4 428.7 %all-gather.33.cloned.1.call-start = ((), (), s32[]{:S(2)}) async-start(), calls=%async_computation.6 | async-start | bytes 4866048 | tf_op jit(solution)/shard_map/all_gather | solution.py:47
  16.1 493.4 %all-gather.35.cloned.1.call-start = ((), (), s32[]{:S(2)}) async-start(), calls=%async_computation.7 | async-start | bytes 4866048 | tf_op jit(solution)/shard_map/all_gather | solution.py:49
  16.9 779.2 %all-reduce.10.cloned.1.call-start = ((), (), s32[]{:S(2)}) async-start(), calls=%async_computation.9 | async-start | bytes 196608 | tf_op jit(solution)/shard_map/psum | solution.py:310
  95.6 165.2 %copy-start.66 = (f32[768]{0:T(1024)}, f32[768]{0:T(1024)S(1)}, u32[]{:S(2)}) copy-start(f32[768]{0:T(1024)S(1)} %get-tuple-element.178) | copy-start | bytes 9220
  145.2 115.6 %copy-start.63 = (f32[3072]{0:T(1024)}, f32[3072]{0:T(1024)S(1)}, u32[]{:S(2)}) copy-start(f32[3072]{0:T(1024)S(1)} %convert_element_type.210) | copy-start | bytes 36868
  188.3 72.5 %copy-start.6 = (f32[1024,768]{1,0:T(8,128)}, f32[1024,768]{1,0:T(8,128)S(1)}, u32[]{:S(2)}) copy-start(f32[1024,768]{1,0:T(8,128)S(1)} %get-tuple-element.263) | copy-start | bytes 9437188
  188.3 72.5 %copy-start.44 = (f32[1024]{0:T(1024)}, f32[1024]{0:T(1024)S(1)}, u32[]{:S(2)}) copy-start(f32[1024]{0:T(1024)S(1)} %broadcast_multiply_fusion.3) | copy-start | bytes 12292
  188.8 72.0 %copy-start.54 = (f32[1024]{0:T(1024)}, f32[1024]{0:T(1024)S(1)}, u32[]{:S(2)}) copy-start(f32[1024]{0:T(1024)S(1)} %fusion.200) | copy-start | bytes 12292
  195.5 65.3 %copy-start.72 = (f32[768]{0:T(1024)S(1)}, f32[768]{0:T(1024)}, u32[]{:S(2)}) copy-start(f32[768]{0:T(1024)} %get-tuple-element.176) | copy-start | bytes 9220
  273.6 103.7 %copy-start.29 = (f32[1024]{0:T(1024)}, f32[1024]{0:T(1024)S(1)}, u32[]{:S(2)}) copy-start(f32[1024]{0:T(1024)S(1)} %broadcast_multiply_fusion.2) | copy-start | bytes 12292
  274.1 103.2 %copy-start.46 = (f32[1024]{0:T(1024)}, f32[1024]{0:T(1024)S(1)}, u32[]{:S(2)}) copy-start(f32[1024]{0:T(1024)S(1)} %fusion.201) | copy-start | bytes 12292
  275.3 54.7 %copy-start.27 = (bf16[1024,16]{0,1:T(8,128)(2,1)}, bf16[1024,16]{0,1:T(8,128)(2,1)S(1)}, u32[]{:S(2)}) copy-start(bf16[1024,16]{0,1:T(8,128)(2,1)S(1)} %convolution_convert_fusion.2) | copy-start | bytes 98308
  377.3 66.8 %copy-start.65 = (f32[3072]{0:T(1024)S(1)}, f32[3072]{0:T(1024)}, u32[]{:S(2)}) copy-start(f32[3072]{0:T(1024)} %convert_element_type.211) | copy-start | bytes 36868
  377.3 66.8 %copy-start.68 = (f32[768]{0:T(1024)S(1)}, f32[768]{0:T(1024)}, u32[]{:S(2)}) copy-start(f32[768]{0:T(1024)} %get-tuple-element.170) | copy-start | bytes 9220
  377.3 66.8 %copy-start.70 = (f32[768]{0:T(1024)S(1)}, f32[768]{0:T(1024)}, u32[]{:S(2)}) copy-start(f32[768]{0:T(1024)} %get-tuple-element.169) | copy-start | bytes 9220
  444.1 65.4 %copy-start.69 = (f32[768]{0:T(1024)S(1)}, f32[768]{0:T(1024)}, u32[]{:S(2)}) copy-start(f32[768]{0:T(1024)} %get-tuple-element.168) | copy-start | bytes 9220
  558.2 83.9 %copy-start.28 = (bf16[1024,16]{0,1:T(8,128)(2,1)S(1)}, bf16[1024,16]{0,1:T(8,128)(2,1)}, u32[]{:S(2)}) copy-start(bf16[1024,16]{0,1:T(8,128)(2,1)} %copy-done.27) | copy-start | bytes 98308
  558.2 88.7 %copy-start.33 = (bf16[2,8,768]{2,1,0:T(8,128)(2,1)S(1)}, bf16[2,8,768]{2,1,0:T(8,128)(2,1)}, u32[]{:S(2)}) copy-start(bf16[2,8,768]{2,1,0:T(8,128)(2,1)} %copy-done.31) | copy-start | bytes 73732
  690.5 82.1 %copy-start.26 = (bf16[1024,16]{0,1:T(8,128)(2,1)S(1)}, bf16[1024,16]{0,1:T(8,128)(2,1)}, u32[]{:S(2)}) copy-start(bf16[1024,16]{0,1:T(8,128)(2,1)} %copy-done.25) | copy-start | bytes 98308
  690.5 86.8 %copy-start.38 = (bf16[2,8,768]{2,1,0:T(8,128)(2,1)S(1)}, bf16[2,8,768]{2,1,0:T(8,128)(2,1)}, u32[]{:S(2)}) copy-start(bf16[2,8,768]{2,1,0:T(8,128)(2,1)} %copy-done.35) | copy-start | bytes 73732
  779.2 128.3 %all-reduce.8.cloned.1.call-start = ((), (), s32[]{:S(2)}) async-start(), calls=%async_computation.8 | async-start | bytes 196608 | tf_op jit(solution)/shard_map/psum | solution.py:309
  796.1 112.9 %copy-start.1 = (bf16[2,80,768]{2,1,0:T(8,128)(2,1)S(1)}, bf16[2,80,768]{2,1,0:T(8,128)(2,1)}, u32[]{:S(2)}) copy-start(bf16[2,80,768]{2,1,0:T(8,128)(2,1)} %param.21) | copy-start | bytes 737284
  (72 other events, 771.4 us)
Sparse Core Ops, SparseCore 0:
  11.5 61.3 all-gather.20
  76.4 52.4 all-gather.22
  131.7 63.7 all-gather.24
  198.3 62.4 all-gather.26
  263.5 57.8 all-gather.28
  324.8 52.4 all-gather.30
  380.2 63.9 all-gather.32
  447.0 62.4 all-gather.34
  779.3 16.7 all-reduce.9
  801.9 105.6 all-reduce.7
